TPU v7x, 32 devices: a whole 2x2x4 slice. The times are simulated.
32 devices in a mesh: row: 4 (over y, core), col: 8 (over z, x).
Axes of the slice: x: 2, y: 2, z: 4, core: 2. Of those that a mesh axis runs over, the one named last changes fastest.
Arguments:
- factor: float32 [6, 2048, 6, 2048], P(None, 'row', None, 'col'), may hold values from -0.0625 to 0.0625
- diag_inv: float32 [6, 2048, 2048], P(None, None, 'row'), may hold values from -2 to 2, as said below
- structure: int32 [6, 6, 16], P(None, None, 'row'), may hold values 0 or 1
- parent: int32 [6], replicated, may hold values from 1 to 6, as said below
- post: float32 [6, 2048, 64], P(None, 'row', 'col'), may hold values from -6 to 6
Outputs:
- mean_x: float32 [6, 2048, 64], P(None, 'row', 'col')
- variance: float32 [6, 2048], P(None, 'row')
Inputs may be any that keep to these rules, and one draw needn't show every extreme that they name: parent[s] > s for s < 5, and parent[5] = 6; every supernode has at most 2 ancestors, and some supernode has exactly that many. The diagonal of each diag_inv[s] lies in 0.5 to 2.
All inputs are finite; a program needn't handle non-finite values. No bound on the sum of `structure` on one device may be relied on, other than what follows from the above.
Results may differ from a plain program's by a relative error of at most 0.00014.
Values sent between devices are 32-bit elements; how exact they have to be, the bound alone decides.
A program may use at most 192 MiB of HBM per device.

v0:
```python
import jax
import jax.numpy as jnp
from jax import lax
from jax.sharding import PartitionSpec as P

LEVELS = 3
HIGHEST = lax.Precision.HIGHEST


def contract(selected, panel_piece):
    return jnp.einsum("tiw,tin->wn", panel_piece, selected, precision=HIGHEST)


def body(factor, diag_inv, structure, parent, post):
    super_count = factor.shape[0]
    row_width = factor.shape[1]
    col_width = factor.shape[3]
    full_width = diag_inv.shape[1]
    rhs_width = post.shape[2]
    row_at = lax.axis_index("row")
    col_at = lax.axis_index("col")
    extended = jnp.concatenate([parent, jnp.full((1,), super_count, jnp.int32)])
    slot_ids = jnp.arange(super_count + 1, dtype=jnp.int32)
    targets = jnp.arange(super_count, dtype=jnp.int32)
    ancestor_hops = []
    current = parent
    for hop_index in range(super_count - 1):
        ancestor_hops.append(current)
        onehot = (current[:, None] == slot_ids[None, :]).astype(jnp.int32)
        current = jnp.sum(onehot * extended[None, :], axis=1)
    ancestry = jnp.zeros((super_count, super_count), jnp.float32)
    for hop_targets in ancestor_hops:
        ancestry = ancestry + (hop_targets[:, None] == targets[None, :]).astype(jnp.float32)
    block_rows = row_width // structure.shape[2]
    row_mask = jnp.repeat(structure.astype(jnp.float32), block_rows, axis=2) * ancestry[:, :, None]
    masked = factor * jnp.transpose(row_mask, (1, 2, 0))[:, :, :, None]
    rows_full = jnp.arange(full_width, dtype=jnp.int32)
    own_cols = row_at * row_width + jnp.arange(row_width, dtype=jnp.int32)
    lower_inv = jnp.where((rows_full[:, None] >= own_cols[None, :])[None, :, :], diag_inv, 0.0)
    unit_cols = col_at * col_width + jnp.arange(col_width, dtype=jnp.int32)
    unit_block = (rows_full[:, None] == unit_cols[None, :]).astype(jnp.float32)
    gathered = lax.all_gather(post, "row", axis=1, tiled=True)
    total_cols = super_count * col_width + rhs_width
    solution = jnp.zeros((super_count, row_width, total_cols), jnp.float32)
    for current_sup in range(super_count - 1, -1, -1):
        later_cols = (current_sup + 1) * col_width
        if current_sup == super_count - 1:
            summed = jnp.zeros((full_width, rhs_width), jnp.float32)
        else:
            picks = []
            chosen_rows = []
            for slot_index in range(LEVELS - 1):
                target = ancestor_hops[slot_index][current_sup]
                is_valid = (target < super_count).astype(jnp.float32)
                clamped = jnp.minimum(target, super_count - 1)
                picks.append(
                    lax.dynamic_index_in_dim(
                        masked[:, :, current_sup, :], clamped, 0, keepdims=False
                    )
                    * is_valid
                )
                chosen_rows.append(
                    lax.dynamic_index_in_dim(solution, clamped, 0, keepdims=False)[:, later_cols:]
                )
            blocks = jnp.stack(picks)
            selected = jnp.stack(chosen_rows)
            partial_value = contract(selected, lax.all_gather(blocks, "col", axis=2, tiled=True))
            summed = lax.psum(partial_value, "row")
        split_at = summed.shape[1] - rhs_width
        remaining = jnp.concatenate(
            [-summed[:, :split_at], gathered[current_sup] - summed[:, split_at:]], axis=1
        )
        right = jnp.concatenate([unit_block, remaining], axis=1)
        fresh = jnp.dot(
            lower_inv[current_sup].T, right, precision=HIGHEST, preferred_element_type=jnp.float32
        )
        solution = solution.at[current_sup, :, current_sup * col_width :].set(fresh)
    mean_x = solution[:, :, super_count * col_width :]
    unit_part = solution[:, :, : super_count * col_width]
    squares = jnp.sum(unit_part * unit_part, axis=2)
    variance = lax.psum(squares, "col")
    return (mean_x, variance)


def solution(mesh):
    return jax.shard_map(
        body,
        mesh=mesh,
        in_specs=(
            P(None, "row", None, "col"),
            P(None, None, "row"),
            P(None, None, "row"),
            P(),
            P(None, "row", "col"),
        ),
        out_specs=(P(None, "row", "col"), P(None, "row")),
        check_vma=False,
    )
```

profile of v0, /device:TPU:0, one launch (start us, length us, event | category | flops | bytes accessed | tf_op | source)
XLA Modules:
  0.0 1485.7 jit_solution(14807575500122001028)
XLA Ops:
  9.6 1.5 fusion.94
  15.8 15.3 %broadcast_multiply_fusion = f32[6,512,6,256]{3,1,2,0:T(8,128)} fusion(f32[6,512,6,256]{3,1,2,0:T(8,128)} %param.17, f32[6,512,6]{1,2,0:T(8,128)S(1)} %multiply_bitcast_fusion.10), kind=kLoop, calls=%fused_computation.18 | loop fusion | flops 4718592 | bytes 37822464 | tf_op jit(solution)/shard_map/mul | solution.py:36
  31.1 10.7 fusion.93
  43.1 8.5 all_gather.18
  53.4 10.7 broadcast_select_fusion
  64.1 8.5 copy-done
  72.5 3.9 fusion.76
  78.6 92.2 %all-gather.6.cloned.1.call-done = f32[2,512,2048]{2,1,0:T(8,128)} async-done(((f32[2,512,256]{2,1,0:T(8,128)}), f32[2,512,2048]{2,1,0:T(8,128)}) %all-gather.6.cloned.1.call-update) | async-done | bytes 8388624 | tf_op jit(solution)/shard_map/all_gather | solution.py:67
  170.8 11.2 convolution_bitcast_fusion.4
  186.9 2.5 multiply_bitcast_fusion.5
  190.5 9.0 scatter.20
  199.4 33.4 %all-reduce.7.cloned.1.call-done = f32[2048,264]{0,1:T(8,128)} async-done(((f32[2048,264]{0,1:T(8,128)}), f32[2048,264]{0,1:T(8,128)}) %all-reduce.7.cloned.1.call-update) | async-done | bytes 2162704 | tf_op jit(solution)/shard_map/psum | solution.py:68
  233.7 1.8 slice_negate_fusion.4
  235.5 9.8 fusion.73
  245.3 3.7 dynamic-slice_bitcast_fusion.7
  251.2 108.7 %all-gather.8.cloned.1.call-done = f32[2,512,2048]{2,1,0:T(8,128)} async-done(((f32[2,512,256]{2,1,0:T(8,128)}), f32[2,512,2048]{2,1,0:T(8,128)}) %all-gather.8.cloned.1.call-update) | async-done | bytes 8388624 | tf_op jit(solution)/shard_map/all_gather | solution.py:67
  359.9 18.0 %convolution_bitcast_fusion.3 = f32[2048,520]{0,1:T(8,128)} fusion(f32[2,512,2048]{2,1,0:T(8,128)} %all-gather.8.cloned.1.call-done, f32[1,512,520]{1,2,0:T(8,128)} %slice_bitcast_fusion.38, f32[1,512,520]{1,2,0:T(8,128)} %slice_bitcast_fusion.39), kind=kOutput, calls=%fused_computation.57 | convolution fusion | flops 13086760960 | bytes 14778368 | tf_op jit(solution)/shard_map/tiw,tin->wn/dot_general | solution.py:11
  380.1 82.8 %all-reduce.9.cloned.1.call-done = f32[2048,520]{0,1:T(8,128)} async-done(((f32[2048,520]{0,1:T(8,128)}), f32[2048,520]{0,1:T(8,128)}) %all-reduce.9.cloned.1.call-update) | async-done | bytes 4259856 | tf_op jit(solution)/shard_map/psum | solution.py:68
  463.7 2.5 slice_negate_fusion.3
  466.3 13.2 bitcast_dynamic-update-slice_fusion
  479.5 3.6 dynamic-slice_bitcast_fusion.5
  483.1 1.3 slice_bitcast_fusion.28
  484.4 1.3 slice_bitcast_fusion.29
  485.7 104.2 %all-gather.10.cloned.1.call-done = f32[2,512,2048]{2,1,0:T(8,128)} async-done(((f32[2,512,256]{2,1,0:T(8,128)}), f32[2,512,2048]{2,1,0:T(8,128)}) %all-gather.10.cloned.1.call-update) | async-done | bytes 8388624 | tf_op jit(solution)/shard_map/all_gather | solution.py:67
  589.9 25.4 %convolution_bitcast_fusion.2 = f32[2048,776]{0,1:T(8,128)} fusion(f32[2,512,2048]{2,1,0:T(8,128)} %all-gather.10.cloned.1.call-done, f32[1,512,776]{1,2,0:T(8,128)} %slice_bitcast_fusion.28, f32[1,512,776]{1,2,0:T(8,128)} %slice_bitcast_fusion.29), kind=kOutput, calls=%fused_computation.56 | convolution fusion | flops 19529474048 | bytes 17924096 | tf_op jit(solution)/shard_map/tiw,tin->wn/dot_general | solution.py:11
  620.4 1.7 multiply_bitcast_fusion.1
  623.3 111.1 %all-reduce.11.cloned.1.call-done = f32[2048,776]{0,1:T(8,128)} async-done(((f32[2048,776]{0,1:T(8,128)}), f32[2048,776]{0,1:T(8,128)}) %all-reduce.11.cloned.1.call-update) | async-done | bytes 6357008 | tf_op jit(solution)/shard_map/psum | solution.py:68
  735.2 3.4 slice_negate_fusion.2
  738.6 17.0 %fusion.53 = f32[6,512,1544]{1,2,0:T(8,128)} fusion(f32[6,512,1544]{1,2,0:T(8,128)} %bitcast_dynamic-update-slice_fusion, f32[2048,8]{0,1:T(8,128)S(1)} %slice_subtract_fusion.2, f32[2048,768]{0,1:T(8,128)S(1)} %slice_negate_fusion.2, f32[2048,256]{0,1:T(8,128)S(1)} %fusion.67, f32[6,2048,512]{2,1,0:T(8,128)} %copy-done), kind=kOutput, calls=%fused_computation.63 | convolution fusion | flops 12989792256 | bytes 14761984 | tf_op jit(solution)/shard_map/dot_general | solution.py:74
  755.5 3.6 dynamic-slice_bitcast_fusion.3
  759.1 1.5 slice_bitcast_fusion.26
  760.6 1.5 slice_bitcast_fusion.27
  762.1 99.4 %all-gather.12.cloned.1.call-done = f32[2,512,2048]{2,1,0:T(8,128)} async-done(((f32[2,512,256]{2,1,0:T(8,128)}), f32[2,512,2048]{2,1,0:T(8,128)}) %all-gather.12.cloned.1.call-update) | async-done | bytes 8388624 | tf_op jit(solution)/shard_map/all_gather | solution.py:67
  861.5 31.5 %convolution_bitcast_fusion.1 = f32[2048,1032]{0,1:T(8,128)} fusion(f32[2,512,2048]{2,1,0:T(8,128)} %all-gather.12.cloned.1.call-done, f32[1,512,1032]{1,2,0:T(8,128)} %slice_bitcast_fusion.26, f32[1,512,1032]{1,2,0:T(8,128)} %slice_bitcast_fusion.27), kind=kOutput, calls=%fused_computation.20 | convolution fusion | flops 25972187136 | bytes 21069824 | tf_op jit(solution)/shard_map/tiw,tin->wn/dot_general | solution.py:11
  894.4 150.9 %all-reduce.13.cloned.1.call-done = f32[2048,1032]{0,1:T(8,128)} async-done(((f32[2048,1032]{0,1:T(8,128)}), f32[2048,1032]{0,1:T(8,128)}) %all-reduce.13.cloned.1.call-update) | async-done | bytes 8454160 | tf_op jit(solution)/shard_map/psum | solution.py:68
  1046.2 4.3 slice_negate_fusion.1
  1050.4 20.4 %fusion.41 = f32[6,512,1544]{1,2,0:T(8,128)} fusion(f32[6,512,1544]{1,2,0:T(8,128)} %fusion.53, f32[2048,8]{0,1:T(8,128)S(1)} %slice_subtract_fusion.1, f32[2048,1024]{0,1:T(8,128)S(1)} %slice_negate_fusion.1, f32[2048,256]{0,1:T(8,128)S(1)} %fusion.67, f32[6,2048,512]{2,1,0:T(8,128)} %copy-done), kind=kOutput, calls=%fused_computation.59 | convolution fusion | flops 16212066304 | bytes 17383424 | tf_op jit(solution)/shard_map/dot_general | solution.py:74
  1070.8 3.6 dynamic-slice_bitcast_fusion.1
  1074.5 1.7 slice_bitcast_fusion.24
  1076.2 1.7 slice_bitcast_fusion.25
  1077.9 94.5 %all-gather.14.cloned.1.call-done = f32[2,512,2048]{2,1,0:T(8,128)} async-done(((f32[2,512,256]{2,1,0:T(8,128)}), f32[2,512,2048]{2,1,0:T(8,128)}) %all-gather.14.cloned.1.call-update) | async-done | bytes 8388624 | tf_op jit(solution)/shard_map/all_gather | solution.py:67
  1172.5 42.1 %convolution_bitcast_fusion = f32[2048,1288]{0,1:T(8,128)} fusion(f32[2,512,2048]{2,1,0:T(8,128)} %all-gather.14.cloned.1.call-done, f32[1,512,1288]{1,2,0:T(8,128)} %slice_bitcast_fusion.24, f32[1,512,1288]{1,2,0:T(8,128)} %slice_bitcast_fusion.25), kind=kOutput, calls=%fused_computation.19 | convolution fusion | flops 32414900224 | bytes 24215552 | tf_op jit(solution)/shard_map/tiw,tin->wn/dot_general | solution.py:11
  1214.6 186.2 %all-reduce.15.cloned.1.call-done = f32[2048,1288]{0,1:T(8,128)} async-done(((f32[2048,1288]{0,1:T(8,128)}), f32[2048,1288]{0,1:T(8,128)}) %all-reduce.15.cloned.1.call-update) | async-done | bytes 10551312 | tf_op jit(solution)/shard_map/psum | solution.py:68
  1400.7 5.1 slice_negate_fusion
  1406.7 23.9 %fusion.47 = f32[6,512,1544]{1,2,0:T(8,128)} fusion(f32[6,512,1544]{1,2,0:T(8,128)} %fusion.41, f32[2048,8]{0,1:T(8,128)S(1)} %slice_subtract_fusion, f32[2048,1280]{0,1:T(8,128)S(1)} %slice_negate_fusion, f32[2048,256]{0,1:T(8,128)S(1)} %fusion.67, f32[6,2048,512]{2,1,0:T(8,128)} %copy-done), kind=kOutput, calls=%fused_computation.61 | convolution fusion | flops 19434340352 | bytes 20004864 | tf_op jit(solution)/shard_map/dot_general | solution.py:74
  1430.6 1.5 slice.382
  1432.1 8.8 fusion
  1440.9 37.7 %psum.47 = f32[6,512]{1,0:T(8,128)} all-reduce(f32[6,512]{1,0:T(8,128)S(1)} %fusion), channel_id=1, replica_groups=mesh['row'=4,'col'=8] {'col'}, use_global_device_ids=true, to_apply=%region_10.11 | all-reduce | flops 3072 | bytes 24576 | tf_op jit(solution)/shard_map/psum | solution.py:81
  (61 shorter events, 21.9 us)
Async XLA Ops:
  7.2 163.6 %all-gather.6.cloned.1.call-start = ((), (), s32[]{:S(2)}) async-start(), calls=%async_computation | async-start | bytes 9437184 | tf_op jit(solution)/shard_map/all_gather | solution.py:67
  41.8 1.3 copy-start.4
  43.0 189.8 %all-reduce.7.cloned.1.call-start = ((), (), s32[]{:S(2)}) async-start(), calls=%async_computation.1 | async-start | bytes 4325376 | tf_op jit(solution)/shard_map/psum | solution.py:68
  51.6 0.8 copy-start.2
  64.1 8.5 copy-start
  182.0 177.9 %all-gather.8.cloned.1.call-start = ((), (), s32[]{:S(2)}) async-start(), calls=%async_computation.2 | async-start | bytes 9437184 | tf_op jit(solution)/shard_map/all_gather | solution.py:67
  190.4 42.4 %copy-start.3 = (f32[6,2048,8]{1,2,0:T(8,128)S(1)}, f32[6,2048,8]{1,2,0:T(8,128)}, u32[]{:S(2)}) copy-start(f32[6,2048,8]{1,2,0:T(8,128)} %copy-done.2) | copy-start | bytes 1179652
  190.4 272.5 %all-reduce.9.cloned.1.call-start = ((), (), s32[]{:S(2)}) async-start(), calls=%async_computation.3 | async-start | bytes 8519680 | tf_op jit(solution)/shard_map/psum | solution.py:68
  378.0 1.0 copy-start.1
  378.0 211.9 %all-gather.10.cloned.1.call-start = ((), (), s32[]{:S(2)}) async-start(), calls=%async_computation.4 | async-start | bytes 9437184 | tf_op jit(solution)/shard_map/all_gather | solution.py:67
  380.0 354.3 %all-reduce.11.cloned.1.call-start = ((), (), s32[]{:S(2)}) async-start(), calls=%async_computation.5 | async-start | bytes 12713984 | tf_op jit(solution)/shard_map/psum | solution.py:68
  615.3 246.2 %all-gather.12.cloned.1.call-start = ((), (), s32[]{:S(2)}) async-start(), calls=%async_computation.6 | async-start | bytes 9437184 | tf_op jit(solution)/shard_map/all_gather | solution.py:67
  623.2 422.1 %all-reduce.13.cloned.1.call-start = ((), (), s32[]{:S(2)}) async-start(), calls=%async_computation.7 | async-start | bytes 16908288 | tf_op jit(solution)/shard_map/psum | solution.py:68
  893.0 279.4 %all-gather.14.cloned.1.call-start = ((), (), s32[]{:S(2)}) async-start(), calls=%async_computation.8 | async-start | bytes 9437184 | tf_op jit(solution)/shard_map/all_gather | solution.py:67
  894.2 506.6 %all-reduce.15.cloned.1.call-start = ((), (), s32[]{:S(2)}) async-start(), calls=%async_computation.9 | async-start | bytes 21102592 | tf_op jit(solution)/shard_map/psum | solution.py:68
Sparse Core Ops, SparseCore 0:
  43.1 127.6 all-gather.5
  182.1 50.6 all-reduce.6
  234.9 124.9 all-gather.7
  378.1 84.7 all-reduce.8
  464.8 125.0 all-gather.9
  615.5 118.8 all-reduce.10
  736.4 125.1 all-gather.11
  893.2 152.0 all-reduce.12
  1047.4 125.0 all-gather.13
  1214.7 185.9 all-reduce.14
where the time goes:
time: 1490 us
  waiting for transfers between devices  1060 us (71%)
  matrix products  216 us (14%)
  other arithmetic  70.2 us (5%)
  local copies, waits for them, and re-layouts  61.6 us (4%)
  blocking collectives  46.2 us (3%)
  between operations  27.1 us (2%)
    psum x5, waiting for transfers between devices, body(): summed = lax.psum(partial_value, 'row')  564 us
    all_gather x5, waiting for transfers between devices, body(): lax.all_gather(blocks, 'col', axis=2, tiled=True)  499 us
    dot_general x5, matrix products, contract(): return jnp.einsum('tiw,tin->wn', panel_piece, selected, precision=HIGHEST)  128 us
    dot_general x6, matrix products, body(): jnp.dot(lower_inv[current_sup].T, right, precision=HIGHEST, preferred_ele...  88.2 us
    psum x1, blocking collectives, body(): variance = lax.psum(squares, 'col')  37.7 us
  transfers between devices with their start and end apart: 10, of which 10 were waited for; matrix products, arithmetic and copies ran while one was open for 9% of the time, Pallas kernels for 0%

commit v1 on v0

--- a/solution.py
+++ b/solution.py
@@ -65,7 +65,11 @@
             blocks = jnp.stack(picks)
             selected = jnp.stack(chosen_rows)
             partial_value = contract(selected, lax.all_gather(blocks, "col", axis=2, tiled=True))
-            summed = lax.psum(partial_value, "row")
+            summed = partial_value
+            for hop in (1, 2):
+                summed = summed + lax.ppermute(
+                    summed, "row", [(dev, dev ^ hop) for dev in range(4)]
+                )
         split_at = summed.shape[1] - rhs_width
         remaining = jnp.concatenate(
             [-summed[:, :split_at], gathered[current_sup] - summed[:, split_at:]], axis=1

time: 1490 us -> 1310 us (0.88)
  waiting for transfers between devices: 1060 us -> 851 us
  other arithmetic: 70.2 us -> 109 us
    ppermute x0 -> x10, waiting for transfers between devices: none -> 721 us  [body(): lax.ppermute(summed, 'row', [(dev, dev ^ hop) for dev in range(4)])]
    psum x5 -> x0, waiting for transfers between devices: 564 us -> none  [body(): summed = lax.psum(partial_value, 'row')]
    all_gather x5, waiting for transfers between devices: 499 us -> 131 us  [body(): lax.all_gather(blocks, 'col', axis=2, tiled=True)]
    add x0 -> x10, other arithmetic: none -> 47.2 us  [body(): summed + lax.ppermute(summed, 'row', [(dev, dev ^ hop) for dev in range(4)])]
  transfers between devices with their start and end apart: 10 -> 15, of which waited for: 10 -> 12; matrix products, arithmetic and copies ran while one was open for 9% -> 15% of each run, Pallas kernels for 0% -> 0%
where the time goes in v1:
time: 1310 us
  waiting for transfers between devices  851 us (65%)
  matrix products  211 us (16%)
  other arithmetic  109 us (8%)
  local copies, waits for them, and re-layouts  58 us (4%)
  blocking collectives  43.2 us (3%)
  between operations  27.4 us (2%)
    ppermute x10, waiting for transfers between devices, body(): lax.ppermute(summed, 'row', [(dev, dev ^ hop) for dev in range(4)])  721 us
    all_gather x5, waiting for transfers between devices, body(): lax.all_gather(blocks, 'col', axis=2, tiled=True)  131 us
    dot_general x5, matrix products, contract(): return jnp.einsum('tiw,tin->wn', panel_piece, selected, precision=HIGHEST)  123 us
    dot_general x6, matrix products, body(): jnp.dot(lower_inv[current_sup].T, right, precision=HIGHEST, preferred_ele...  88.6 us
    add x10, other arithmetic, body(): summed + lax.ppermute(summed, 'row', [(dev, dev ^ hop) for dev in range(4)])  47.2 us
    psum x1, blocking collectives, body(): variance = lax.psum(squares, 'col')  34.8 us
  transfers between devices with their start and end apart: 15, of which 12 were waited for; matrix products, arithmetic and copies ran while one was open for 15% of the time, Pallas kernels for 0%

profile of v1, /device:TPU:0, one launch (start us, length us, event | category | flops | bytes accessed | tf_op | source)
XLA Modules:
  0.0 1308.9 jit_solution(8952671878666658900)
XLA Ops:
  16.0 15.3 %broadcast_multiply_fusion = f32[6,512,6,256]{3,1,2,0:T(8,128)} fusion(f32[6,512,6,256]{3,1,2,0:T(8,128)} %param.17, f32[6,512,6]{1,2,0:T(8,128)S(1)} %multiply_bitcast_fusion.10), kind=kLoop, calls=%fused_computation.18 | loop fusion | flops 4718592 | bytes 37822464 | tf_op jit(solution)/shard_map/mul | solution.py:36
  31.3 10.8 fusion.93
  49.6 2.3 multiply_bitcast_fusion.5
  53.0 8.3 all_gather.18
  62.4 10.9 broadcast_select_fusion
  73.4 8.4 copy-done
  81.8 4.0 fusion.76
  87.1 85.1 %all-gather.6.cloned.1.call-done = f32[2,512,2048]{2,1,0:T(8,128)} async-done(((f32[2,512,256]{2,1,0:T(8,128)}), f32[2,512,2048]{2,1,0:T(8,128)}) %all-gather.6.cloned.1.call-update) | async-done | bytes 8388624 | tf_op jit(solution)/shard_map/all_gather | solution.py:67
  172.2 10.0 convolution_bitcast_fusion.4
  182.4 4.2 collective-permute-done
  189.9 8.9 scatter.20
  198.8 37.4 %collective-permute-done.1 = f32[2048,264]{0,1:T(8,128)} collective-permute-done((f32[2048,264]{0,1:T(8,128)S(1)}, f32[2048,264]{0,1:T(8,128)}, u32[]{:S(2)}, u32[]{:S(2)}) %collective-permute-start.1) | collective-permute-done | bytes 2162720 | tf_op jit(solution)/shard_map/ppermute | solution.py:70
  236.2 1.9 add.147
  238.4 9.6 fusion.73
  248.0 3.6 dynamic-slice_bitcast_fusion.7
  251.7 45.7 %all-gather.8.cloned.1.call-done = f32[2,512,2048]{2,1,0:T(8,128)} async-done(((f32[2,512,256]{2,1,0:T(8,128)}), f32[2,512,2048]{2,1,0:T(8,128)}) %all-gather.8.cloned.1.call-update) | async-done | bytes 8388624 | tf_op jit(solution)/shard_map/all_gather | solution.py:67
  297.4 16.5 %convolution_bitcast_fusion.3 = f32[2048,520]{0,1:T(8,128)S(1)} fusion(f32[2,512,2048]{2,1,0:T(8,128)} %all-gather.8.cloned.1.call-done, f32[1,512,520]{1,2,0:T(8,128)S(1)} %slice_bitcast_fusion.38, f32[1,512,520]{1,2,0:T(8,128)S(1)} %slice_bitcast_fusion.39), kind=kOutput, calls=%fused_computation.57 | convolution fusion | flops 13086760960 | bytes 14778368 | tf_op jit(solution)/shard_map/tiw,tin->wn/dot_general | solution.py:11
  314.0 7.2 collective-permute-done.2
  323.9 92.5 %collective-permute-done.3 = f32[2048,520]{0,1:T(8,128)S(1)} collective-permute-done((f32[2048,520]{0,1:T(8,128)S(1)}, f32[2048,520]{0,1:T(8,128)S(1)}, u32[]{:S(2)}, u32[]{:S(2)}) %collective-permute-start.3) | collective-permute-done | bytes 4259872 | tf_op jit(solution)/shard_map/ppermute | solution.py:70
  419.1 12.8 bitcast_dynamic-update-slice_fusion
  431.9 3.6 dynamic-slice_bitcast_fusion.5
  438.1 25.7 %convolution_bitcast_fusion.2 = f32[2048,776]{0,1:T(8,128)} fusion(f32[2,512,2048]{2,1,0:T(8,128)} %all-gather.10.cloned.1.call-done, f32[1,512,776]{1,2,0:T(8,128)} %slice_bitcast_fusion.28, f32[1,512,776]{1,2,0:T(8,128)} %slice_bitcast_fusion.29), kind=kOutput, calls=%fused_computation.56 | convolution fusion | flops 19529474048 | bytes 17924096 | tf_op jit(solution)/shard_map/tiw,tin->wn/dot_general | solution.py:11
  469.0 1.7 multiply_bitcast_fusion.1
  471.7 2.6 collective-permute-done.4
  474.3 6.7 add.154
  482.5 137.6 %collective-permute-done.5 = f32[2048,776]{0,1:T(8,128)} collective-permute-done((f32[2048,776]{0,1:T(8,128)S(1)}, f32[2048,776]{0,1:T(8,128)}, u32[]{:S(2)}, u32[]{:S(2)}) %collective-permute-start.5) | collective-permute-done | bytes 6357024 | tf_op jit(solution)/shard_map/ppermute | solution.py:70
  620.1 4.1 add.155
  625.4 17.0 %fusion.53 = f32[6,512,1544]{1,2,0:T(8,128)} fusion(f32[6,512,1544]{1,2,0:T(8,128)} %bitcast_dynamic-update-slice_fusion, f32[2048,8]{0,1:T(8,128)S(1)} %slice_subtract_fusion.2, f32[2048,768]{0,1:T(8,128)S(1)} %slice_negate_fusion.2, f32[2048,256]{0,1:T(8,128)S(1)} %copy-done.3, f32[6,2048,512]{2,1,0:T(8,128)} %copy-done), kind=kOutput, calls=%fused_computation.63 | convolution fusion | flops 12989792256 | bytes 14761984 | tf_op jit(solution)/shard_map/dot_general | solution.py:78
  642.4 3.6 dynamic-slice_bitcast_fusion.3
  648.9 31.9 %convolution_bitcast_fusion.1 = f32[2048,1032]{0,1:T(8,128)} fusion(f32[2,512,2048]{2,1,0:T(8,128)} %all-gather.12.cloned.1.call-done, f32[1,512,1032]{1,2,0:T(8,128)} %slice_bitcast_fusion.26, f32[1,512,1032]{1,2,0:T(8,128)} %slice_bitcast_fusion.27), kind=kOutput, calls=%fused_computation.20 | convolution fusion | flops 25972187136 | bytes 21069824 | tf_op jit(solution)/shard_map/tiw,tin->wn/dot_general | solution.py:11
  681.9 12.5 collective-permute-done.6
  694.5 12.1 add.158
  708.1 182.7 %collective-permute-done.7 = f32[2048,1032]{0,1:T(8,128)} collective-permute-done((f32[2048,1032]{0,1:T(8,128)}, f32[2048,1032]{0,1:T(8,128)}, u32[]{:S(2)}, u32[]{:S(2)}) %collective-permute-start.7) | collective-permute-done | bytes 8454176 | tf_op jit(solution)/shard_map/ppermute | solution.py:70
  890.8 12.1 add.159
  903.7 4.3 slice_negate_fusion.1
  908.0 20.4 %fusion.41 = f32[6,512,1544]{1,2,0:T(8,128)} fusion(f32[6,512,1544]{1,2,0:T(8,128)} %fusion.53, f32[2048,8]{0,1:T(8,128)S(1)} %slice_subtract_fusion.1, f32[2048,1024]{0,1:T(8,128)S(1)} %slice_negate_fusion.1, f32[2048,256]{0,1:T(8,128)S(1)} %copy-done.3, f32[6,2048,512]{2,1,0:T(8,128)} %copy-done), kind=kOutput, calls=%fused_computation.59 | convolution fusion | flops 16212066304 | bytes 17383424 | tf_op jit(solution)/shard_map/dot_general | solution.py:78
  928.4 3.6 dynamic-slice_bitcast_fusion.1
  932.0 1.8 slice_bitcast_fusion.24
  933.8 1.7 slice_bitcast_fusion.25
  935.5 38.5 %convolution_bitcast_fusion = f32[2048,1288]{0,1:T(8,128)S(1)} fusion(f32[2,512,2048]{2,1,0:T(8,128)} %all-gather.14.cloned.1.call-done, f32[1,512,1288]{1,2,0:T(8,128)} %slice_bitcast_fusion.24, f32[1,512,1288]{1,2,0:T(8,128)} %slice_bitcast_fusion.25), kind=kOutput, calls=%fused_computation.19 | convolution fusion | flops 32414900224 | bytes 24215552 | tf_op jit(solution)/shard_map/tiw,tin->wn/dot_general | solution.py:11
  974.1 16.2 %collective-permute-done.8 = f32[2048,1288]{0,1:T(8,128)S(1)} collective-permute-done((f32[2048,1288]{0,1:T(8,128)S(1)}, f32[2048,1288]{0,1:T(8,128)S(1)}, u32[]{:S(2)}, u32[]{:S(2)}) %collective-permute-start.8) | collective-permute-done | bytes 10551328 | tf_op jit(solution)/shard_map/ppermute | solution.py:70
  990.3 2.5 add.162
  994.4 227.5 %collective-permute-done.9 = f32[2048,1288]{0,1:T(8,128)} collective-permute-done((f32[2048,1288]{0,1:T(8,128)S(1)}, f32[2048,1288]{0,1:T(8,128)}, u32[]{:S(2)}, u32[]{:S(2)}) %collective-permute-start.9) | collective-permute-done | bytes 10551328 | tf_op jit(solution)/shard_map/ppermute | solution.py:70
  1221.8 5.3 add.163
  1227.2 5.1 slice_negate_fusion
  1232.3 24.7 %fusion.47 = f32[6,512,1544]{1,2,0:T(8,128)} fusion(f32[6,512,1544]{1,2,0:T(8,128)} %fusion.41, f32[2048,8]{0,1:T(8,128)S(1)} %slice_subtract_fusion, f32[2048,1280]{0,1:T(8,128)} %slice_negate_fusion, f32[2048,256]{0,1:T(8,128)S(1)} %copy-done.3, f32[6,2048,512]{2,1,0:T(8,128)} %copy-done), kind=kOutput, calls=%fused_computation.61 | convolution fusion | flops 19434340352 | bytes 20004864 | tf_op jit(solution)/shard_map/dot_general | solution.py:78
  1258.5 8.8 fusion
  1267.3 34.8 %psum.7 = f32[6,512]{1,0:T(8,128)} all-reduce(f32[6,512]{1,0:T(8,128)S(1)} %fusion), channel_id=1, replica_groups=mesh['row'=4,'col'=8] {'col'}, use_global_device_ids=true, to_apply=%region_5.6 | all-reduce | flops 3072 | bytes 24576 | tf_op jit(solution)/shard_map/psum | solution.py:85
  (78 shorter events, 36.9 us)
Async XLA Ops:
  7.2 165.1 %all-gather.6.cloned.1.call-start = ((), (), s32[]{:S(2)}) async-start(), calls=%async_computation | async-start | bytes 9437184 | tf_op jit(solution)/shard_map/all_gather | solution.py:67
  44.4 253.0 %all-gather.8.cloned.1.call-start = ((), (), s32[]{:S(2)}) async-start(), calls=%async_computation.1 | async-start | bytes 9437184 | tf_op jit(solution)/shard_map/all_gather | solution.py:67
  52.9 385.1 %all-gather.10.cloned.1.call-start = ((), (), s32[]{:S(2)}) async-start(), calls=%async_computation.2 | async-start | bytes 9437184 | tf_op jit(solution)/shard_map/all_gather | solution.py:67
  62.4 11.0 copy-start.1
  73.4 8.4 copy-start
  182.3 6.3 copy-start.4
  182.3 6.3 copy-start.5
  182.3 4.3 collective-permute-start
  187.0 49.2 %collective-permute-start.1 = (f32[2048,264]{0,1:T(8,128)S(1)}, f32[2048,264]{0,1:T(8,128)}, u32[]{:S(2)}, u32[]{:S(2)}) collective-permute-start(f32[2048,264]{0,1:T(8,128)S(1)} %add.146), channel_id=1, source_target_pairs={{0,16},{8,24},{16,0},{24,8},{1,17},{9,25},{17,1},{25,9},{2,18},{10... | collective-permute-start | bytes 6488072 | tf_op jit(solution)/shard_map/ppermute | solution.py:70
  189.7 459.3 %all-gather.12.cloned.1.call-start = ((), (), s32[]{:S(2)}) async-start(), calls=%async_computation.3 | async-start | bytes 9437184 | tf_op jit(solution)/shard_map/all_gather | solution.py:67
  198.8 39.5 %copy-start.2 = (f32[2048,256]{0,1:T(8,128)S(1)}, f32[2048,256]{0,1:T(8,128)}, u32[]{:S(2)}) copy-start(f32[2048,256]{0,1:T(8,128)} %copy-done.1) | copy-start | bytes 6291460
  313.9 7.3 collective-permute-start.2
  322.3 94.1 %collective-permute-start.3 = (f32[2048,520]{0,1:T(8,128)S(1)}, f32[2048,520]{0,1:T(8,128)S(1)}, u32[]{:S(2)}, u32[]{:S(2)}) collective-permute-start(f32[2048,520]{0,1:T(8,128)S(1)} %add.150), channel_id=1, source_target_pairs={{0,16},{8,24},{16,0},{24,8},{1,17},{9,25},{17,1},{25,9},{2,18},{10... | collective-permute-start | bytes 12779528 | tf_op jit(solution)/shard_map/ppermute | solution.py:70
  417.5 1.6 copy-start.3
  463.7 10.6 collective-permute-start.4
  471.7 463.8 %all-gather.14.cloned.1.call-start = ((), (), s32[]{:S(2)}) async-start(), calls=%async_computation.4 | async-start | bytes 9437184 | tf_op jit(solution)/shard_map/all_gather | solution.py:67
  481.0 139.1 %collective-permute-start.5 = (f32[2048,776]{0,1:T(8,128)S(1)}, f32[2048,776]{0,1:T(8,128)}, u32[]{:S(2)}, u32[]{:S(2)}) collective-permute-start(f32[2048,776]{0,1:T(8,128)S(1)} %add.154), channel_id=1, source_target_pairs={{0,16},{8,24},{16,0},{24,8},{1,17},{9,25},{17,1},{25,9},{2,18},{10... | collective-permute-start | bytes 19070984 | tf_op jit(solution)/shard_map/ppermute | solution.py:70
  680.8 13.7 %collective-permute-start.6 = (f32[2048,1032]{0,1:T(8,128)}, f32[2048,1032]{0,1:T(8,128)}, u32[]{:S(2)}, u32[]{:S(2)}) collective-permute-start(f32[2048,1032]{0,1:T(8,128)} %convolution_bitcast_fusion.1), channel_id=1, source_target_pairs={{0,8},{8,0},{16,24},{24,16},{1,9},{9,1},{17,25},{25,17},{2,10},{10... | collective-permute-start | bytes 25362440 | tf_op jit(solution)/shard_map/ppermute | solution.py:70
  706.6 184.2 %collective-permute-start.7 = (f32[2048,1032]{0,1:T(8,128)}, f32[2048,1032]{0,1:T(8,128)}, u32[]{:S(2)}, u32[]{:S(2)}) collective-permute-start(f32[2048,1032]{0,1:T(8,128)} %add.158), channel_id=1, source_target_pairs={{0,16},{8,24},{16,0},{24,8},{1,17},{9,25},{17,1},{25,9},{2,18},{10... | collective-permute-start | bytes 25362440 | tf_op jit(solution)/shard_map/ppermute | solution.py:70
  974.0 16.3 %collective-permute-start.8 = (f32[2048,1288]{0,1:T(8,128)S(1)}, f32[2048,1288]{0,1:T(8,128)S(1)}, u32[]{:S(2)}, u32[]{:S(2)}) collective-permute-start(f32[2048,1288]{0,1:T(8,128)S(1)} %convolution_bitcast_fusion), channel_id=1, source_target_pairs={{0,8},{8,0},{16,24},{24,16},{1,9},{9,1},{17,25},{25,17},{2,10},{10... | collective-permute-start | bytes 31653896 | tf_op jit(solution)/shard_map/ppermute | solution.py:70
  992.8 229.0 %collective-permute-start.9 = (f32[2048,1288]{0,1:T(8,128)S(1)}, f32[2048,1288]{0,1:T(8,128)}, u32[]{:S(2)}, u32[]{:S(2)}) collective-permute-start(f32[2048,1288]{0,1:T(8,128)S(1)} %add.162), channel_id=1, source_target_pairs={{0,16},{8,24},{16,0},{24,8},{1,17},{9,25},{17,1},{25,9},{2,18},{10... | collective-permute-start | bytes 31653896 | tf_op jit(solution)/shard_map/ppermute | solution.py:70
Sparse Core Ops, SparseCore 0:
  44.5 127.6 all-gather.5
  174.3 123.1 all-gather.7
  299.5 123.1 all-gather.9
  471.8 123.2 all-gather.11
  682.0 123.1 all-gather.13
